TPU v7x, 256 devices: a whole 4x4x8 slice. The times are simulated.
256 devices in a mesh: song: 4 (over y), seq: 64 (over z, x, core).
Axes of the slice: x: 4, y: 4, z: 8, core: 2. Of those that a mesh axis runs over, the one named last changes fastest.
Arguments:
- queries: bfloat16 [4, 8192, 2048], P('song', 'seq'), may hold values from -64 to 64
- keys: bfloat16 [4, 8192, 2048], P('song', 'seq'), may hold values from -64 to 64
- values: bfloat16 [4, 8192, 2048], P('song', 'seq'), may hold values from -6 to 6
- lyric_keys: bfloat16 [4, 384, 2048], P('song', 'seq'), may hold values from -64 to 64
- lyric_values: bfloat16 [4, 384, 2048], P('song', 'seq'), may hold values from -6 to 6
- q_gain: float32 [128], replicated, may hold values from 0.5 to 1.5
- k_gain: float32 [128], replicated, may hold values from 0.5 to 1.5
- cotangent: bfloat16 [4, 8192, 2048], P('song', 'seq'), may hold values from -12 to 12
- alignment: int32 [4, 64, 2], P('song', 'seq'), may hold values from -1 to 2, as said below
- lyric_len: int32 [4], P('song'), may hold values from 192 to 384
Outputs:
- attn_out: bfloat16 [4, 8192, 2048], P('song', 'seq')
- grad_queries: bfloat16 [4, 8192, 2048], P('song', 'seq')
- grad_keys: bfloat16 [4, 8192, 2048], P('song', 'seq')
- grad_values: bfloat16 [4, 8192, 2048], P('song', 'seq')
- grad_lyric_keys: bfloat16 [4, 384, 2048], P('song', 'seq')
- grad_lyric_values: bfloat16 [4, 384, 2048], P('song', 'seq')
- grad_q_gain: float32 [128], replicated
- grad_k_gain: float32 [128], replicated
Inputs may be any that keep to these rules, and one draw needn't show every extreme that they name: `alignment`: in each row the entries that are not -1 are distinct.
All inputs are finite; a program needn't handle non-finite values.
Results may differ from a plain program's by a relative error of at most 0.01.
Values may be sent and summed in bfloat16 or wider, within the bound.
A program may use at most 128 MiB of HBM per device.

v0:
```python
import jax
import jax.numpy as jnp
from jax import lax
from jax.sharding import PartitionSpec as P

BLK = 128
WIN = 1
TILES = 2
NORM_EPS = 1e-06


def extended_2(block, sides, width):
    for axis, dim in sides:
        count = lax.axis_size(axis)
        forward = [(i, i + 1) for i in range(count - 1)]
        backward = [(target, source) for source, target in forward]
        low = lax.ppermute(
            lax.slice_in_dim(block, block.shape[dim] - width, None, axis=dim), axis, forward
        )
        high = lax.ppermute(lax.slice_in_dim(block, 0, width, axis=dim), axis, backward)
        block = jnp.concatenate([low, block, high], axis=dim)
    return block


def norm_heads(inputs, norm_gain):
    row_values = inputs.astype(jnp.float32).reshape(inputs.shape[0], -1, norm_gain.shape[0])
    inverse = lax.rsqrt(jnp.mean(row_values * row_values, axis=-1, keepdims=True) + NORM_EPS)
    return (row_values * inverse * norm_gain, inverse)


def norm_back(inputs, inverse, norm_gain, grad_out):
    row_values = inputs.astype(jnp.float32).reshape(grad_out.shape)
    scaled = grad_out * norm_gain
    grad_input = inverse * scaled - row_values * inverse * inverse * inverse * jnp.mean(
        scaled * row_values, axis=-1, keepdims=True
    )
    grad_gain = jnp.sum(grad_out * row_values * inverse, axis=(0, 1))
    return (grad_input.reshape(inputs.shape), grad_gain)


def block_pass(query_rows, key_rows, value_rows, keep_mask, grad_rows, score_scale):
    scores = (
        jnp.einsum("qhd,khd->hqk", query_rows, key_rows, preferred_element_type=jnp.float32)
        * score_scale
    )
    exp_scores = jnp.where(keep_mask[None, None, :], jnp.exp(scores), 0.0)
    totals = jnp.sum(exp_scores, axis=2)
    prob_full = exp_scores / totals[:, :, None]
    prob_low = prob_full.astype(jnp.bfloat16)
    block_output = jnp.einsum(
        "hqk,khd->qhd", prob_low, value_rows, preferred_element_type=jnp.float32
    ).astype(jnp.bfloat16)
    delta_rows = jnp.sum(grad_rows.astype(jnp.float32) * block_output.astype(jnp.float32), axis=2).T
    grad_prob = jnp.einsum(
        "qhd,khd->hqk", grad_rows, value_rows, preferred_element_type=jnp.float32
    )
    grad_score = (prob_full * (grad_prob - delta_rows[:, :, None])).astype(jnp.bfloat16)
    query_gradient = (
        jnp.einsum("hqk,khd->qhd", grad_score, key_rows, preferred_element_type=jnp.float32)
        * score_scale
    )
    grad_key = (
        jnp.einsum("hqk,qhd->khd", grad_score, query_rows, preferred_element_type=jnp.float32)
        * score_scale
    )
    value_gradient = jnp.einsum(
        "hqk,qhd->khd", prob_low, grad_rows, preferred_element_type=jnp.float32
    )
    return (block_output, query_gradient, grad_key, value_gradient)


def body(
    queries, keys, values, lyric_keys, lyric_values, q_gain, k_gain, cotangent, alignment, lyric_len
):
    head_size = q_gain.shape[0]
    model_width = queries.shape[2]
    head_count = model_width // head_size
    frames = queries.shape[1]
    lyric_local = lyric_keys.shape[1]
    seq_count = lax.axis_size("seq")
    border_rows = WIN * BLK
    window_extent = (2 * WIN + 1) * BLK
    score_scale = head_size ** (-0.5)
    total_frames = frames * seq_count
    first_frame = lax.axis_index("seq") * frames
    lyric_total = lyric_local * seq_count
    lyric_blocks = lyric_total // BLK
    lyric_pair = jnp.stack([lyric_keys[0], lyric_values[0]])
    lyric_all = lax.all_gather(lyric_pair, "seq", axis=1, tiled=True)
    lyric_raw_all = lyric_all[0]
    lyric_val_all = lyric_all[1].reshape(lyric_total, head_count, head_size)
    query_raw = queries[0]
    key_raw = keys[0]
    query_full, query_inv = norm_heads(query_raw, q_gain)
    key_full, key_inv = norm_heads(key_raw, k_gain)
    lyric_full_all, lyric_inv_all = norm_heads(lyric_raw_all, k_gain)
    lyric_inv = norm_heads(lyric_keys[0], k_gain)[1]
    query_norm = query_full.astype(jnp.bfloat16)
    key_norm = key_full.astype(jnp.bfloat16)
    lyric_key_all = lyric_full_all.astype(jnp.bfloat16)
    stacked = jnp.stack([key_norm.reshape(frames, model_width), values[0]])
    extended = extended_2(stacked, (("seq", 1),), border_rows)
    ext_keys = extended[0].reshape(frames + 2 * border_rows, head_count, head_size)
    ext_vals = extended[1].reshape(frames + 2 * border_rows, head_count, head_size)
    grad_heads = cotangent[0].reshape(frames, head_count, head_size)
    length = lyric_len[0]
    position = first_frame - border_rows + jnp.arange(window_extent, dtype=jnp.int32)
    audio_mask = (position >= 0) & (position < total_frames)
    tile_ids = alignment[0, 0]
    starts = [jnp.maximum(tile_ids[s], 0) * BLK for s in range(TILES)]
    slot_keys = [lax.dynamic_slice_in_dim(lyric_key_all, st, BLK, 0) for st in starts]
    slot_vals = [lax.dynamic_slice_in_dim(lyric_val_all, st, BLK, 0) for st in starts]
    lyric_mask = jnp.concatenate(
        [
            (tile_ids[s] >= 0) & (starts[s] + jnp.arange(BLK, dtype=jnp.int32) < length)
            for s in range(TILES)
        ]
    )
    all_keys = jnp.concatenate([ext_keys] + slot_keys, axis=0)
    all_vals = jnp.concatenate([ext_vals] + slot_vals, axis=0)
    keep_mask = jnp.concatenate([audio_mask, lyric_mask], axis=0)
    block_output, grad_qn, grad_key, value_gradient = block_pass(
        query_norm, all_keys, all_vals, keep_mask, grad_heads, score_scale
    )
    lyric_gk = grad_key[window_extent:].reshape(TILES, BLK, head_count, head_size)
    lyric_gv = value_gradient[window_extent:].reshape(TILES, BLK, head_count, head_size)
    block_ids = jnp.arange(lyric_blocks, dtype=jnp.int32)
    pick = [(tile_ids[s] == block_ids)[:, None, None, None] for s in range(TILES)]
    part_gk = sum((jnp.where(pick[s], lyric_gk[s][None], 0.0) for s in range(TILES)))
    part_gv = sum((jnp.where(pick[s], lyric_gv[s][None], 0.0) for s in range(TILES)))
    lyric_scaled_all = lyric_raw_all.astype(jnp.float32).reshape(
        lyric_blocks, BLK, head_count, head_size
    ) * lyric_inv_all.reshape(lyric_blocks, BLK, head_count, 1)
    lyric_gain_vector = jnp.sum(part_gk * lyric_scaled_all, axis=(0, 1, 2))
    parts = jnp.stack([part_gk, part_gv]).reshape(2, seq_count, lyric_local * model_width)
    summed = lax.psum_scatter(parts, "seq", scatter_dimension=1, tiled=True)
    summed_key = summed[0].reshape(lyric_local, head_count, head_size)
    summed_val = summed[1].reshape(lyric_local, model_width)
    ext_grad_key = grad_key[:window_extent]
    ext_grad_val = value_gradient[:window_extent]
    own_grad_key = ext_grad_key[border_rows : border_rows + frames]
    own_grad_val = ext_grad_val[border_rows : border_rows + frames]
    rims = jnp.stack(
        [
            jnp.concatenate(
                [ext_grad_key[:border_rows], ext_grad_key[border_rows + frames :]], axis=0
            ).reshape(2 * border_rows, model_width),
            jnp.concatenate(
                [ext_grad_val[:border_rows], ext_grad_val[border_rows + frames :]], axis=0
            ).reshape(2 * border_rows, model_width),
        ]
    )
    received = extended_2(rims.astype(jnp.bfloat16), (("seq", 1),), border_rows).astype(rims.dtype)
    from_left = received[:, :border_rows].reshape(2, border_rows, head_count, head_size)
    from_right = received[:, 3 * border_rows :].reshape(2, border_rows, head_count, head_size)
    own_grad_key = (
        own_grad_key.at[:border_rows]
        .add(from_left[0])
        .at[frames - border_rows :]
        .add(from_right[0])
    )
    own_grad_val = (
        own_grad_val.at[:border_rows]
        .add(from_left[1])
        .at[frames - border_rows :]
        .add(from_right[1])
    )
    unnormed_query_gradient, query_gain_vector = norm_back(
        query_raw, query_inv, q_gain, grad_qn.reshape(frames, head_count, head_size)
    )
    unnormed_key_gradient, key_gain_vector = norm_back(key_raw, key_inv, k_gain, own_grad_key)
    total_gains = lax.psum(
        jnp.stack([query_gain_vector, key_gain_vector + lyric_gain_vector]), ("song", "seq")
    )
    unnormed_lyric_gradient = norm_back(lyric_keys[0], lyric_inv, k_gain, summed_key)[0]
    return (
        block_output.reshape(1, frames, model_width),
        unnormed_query_gradient.astype(jnp.bfloat16)[None],
        unnormed_key_gradient.astype(jnp.bfloat16)[None],
        own_grad_val.reshape(1, frames, model_width).astype(jnp.bfloat16),
        unnormed_lyric_gradient.astype(jnp.bfloat16)[None],
        summed_val.astype(jnp.bfloat16)[None],
        total_gains[0],
        total_gains[1],
    )


def solution(mesh):
    in_specs = (
        P("song", "seq", None),
        P("song", "seq", None),
        P("song", "seq", None),
        P("song", "seq", None),
        P("song", "seq", None),
        P(),
        P(),
        P("song", "seq", None),
        P("song", "seq", None),
        P("song"),
    )
    out_specs = (
        P("song", "seq", None),
        P("song", "seq", None),
        P("song", "seq", None),
        P("song", "seq", None),
        P("song", "seq", None),
        P("song", "seq", None),
        P(),
        P(),
    )
    return jax.shard_map(body, mesh=mesh, in_specs=in_specs, out_specs=out_specs, check_vma=False)
```

profile of v0, /device:TPU:8, one launch (start us, length us, event | category | flops | bytes accessed | tf_op | source)
XLA Modules:
  0.0 408.7 jit_solution(17352905032902719818)
XLA Ops:
  7.2 0.8 copy.161
  8.0 0.8 copy.160
  8.8 0.7 pad_maximum_fusion.15
  9.6 1.3 copy.159
  11.0 1.4 copy.158
  12.3 0.7 broadcast_bitcast_fusion
  13.0 1.1 multiply_reduce_fusion.6
  14.6 1.3 collective-permute-start.1
  15.9 4.0 collective-permute-start
  23.1 1.0 copy.168
  24.8 1.2 copy.163
  26.2 2.0 pad_maximum_fusion.1
  28.2 1.5 fusion.42
  29.7 1.6 copy.166
  31.3 61.3 %all-gather.2.cloned.1.call-done = bf16[2,384,2048]{2,0,1:T(2,128)(2,1)} async-done(((bf16[2,6,2048]{2,0,1:T(2,128)(2,1)}), bf16[2,384,2048]{2,0,1:T(2,128)(2,1)}) %all-gather.2.cloned.1.call-update) | async-done | bytes 3145744 | tf_op jit(solution)/shard_map/all_gather | solution.py:89
  92.6 9.6 %fusion.43 = (bf16[1,384,2048]{2,0,1:T(2,128)(2,1)}, bf16[1,384,2048]{2,0,1:T(2,128)(2,1)}) fusion(bf16[2,384,2048]{2,0,1:T(2,128)(2,1)} %all-gather.2.cloned.1.call-done), kind=kLoop, calls=%fused_computation.109 | loop fusion | bytes 6291456 | tf_op jit(solution)/shard_map/slice | solution.py:90
  102.1 6.9 %copy.192 = bf16[1,384,2048]{1,2,0:T(8,128)(2,1)S(1)} copy(bf16[1,384,2048]{2,0,1:T(2,128)(2,1)} %get-tuple-element.169) | data formatting | bytes 3145728
  109.1 2.1 copy.165
  111.6 6.9 %copy.162 = bf16[1,384,2048]{1,2,0:T(8,128)(2,1)S(1)} copy(bf16[1,384,2048]{2,0,1:T(2,128)(2,1)} %get-tuple-element.170) | data formatting | bytes 3145728 | tf_op jit(solution)/shard_map/slice | solution.py:91
  118.5 2.4 multiply_convert_fusion
  121.3 1.4 copy-done.9
  122.7 1.6 fusion.2
  124.3 3.1 fusion.48
  127.5 2.4 multiply_reduce_fusion.4
  129.9 2.2 fusion
  132.1 3.3 fusion.47
  136.3 1.7 fusion.11
  138.0 1.3 collective-permute-start.3
  139.3 4.0 collective-permute-start.2
  143.9 1.3 iota_compare_fusion
  145.3 3.3 maximum_convert_fusion
  148.9 1.7 fusion.40
  150.6 1.4 copy.174
  152.0 1.4 copy.173
  153.4 3.7 fusion.41
  157.1 1.4 copy.176
  158.5 1.4 copy.175
  159.9 4.5 %select_add_fusion.1 = (f32[3,128,16,128]{3,2,1,0:T(8,128)S(1)}, f32[3,128,16,128]{3,2,1,0:T(8,128)}) fusion(f32[128,16,128]{2,1,0:T(8,128)} %copy.174, f32[128,16,128]{2,1,0:T(8,128)} %copy.173, pred[3]{0:T(512)(128)(4,1)S(1)} %get-tuple-element.198, pred[3]{0:T(512)(128)(4,1)S(1)} %get-tuple-element.199, f32[128,16,128]{2,1,0:T(8,128)} %copy.176, ...), kind=kLoop, calls=%fused_computation.10 | loop fusion | flops 4718592 | bytes 10485766 | tf_op jit(solution)/shard_map/add | solution.py:129
  164.5 4.3 %add.181 = f32[1,64,12288]{2,1,0:T(8,128)} reshape(f32[3,128,16,128]{3,2,1,0:T(8,128)} %get-tuple-element.184) | data formatting | bytes 6291456 | tf_op jit(solution)/shard_map/add | solution.py:130
  168.8 1.9 add.179
  170.7 3.3 pad_maximum_fusion
  174.0 7.5 %copy.177 = f32[2,64,12288]{2,0,1:T(2,128)} copy(f32[2,64,12288]{2,1,0:T(8,128)S(1)} %pad_maximum_fusion) | data formatting | bytes 12582912 | tf_op jit(solution)/shard_map/stack | solution.py:135
  181.6 0.6 copy-done.17
  182.5 1.0 copy.182
  183.6 3.2 fusion.16
  187.1 1.0 copy.183
  188.1 0.9 mul.399
  189.0 2.3 mul.400
  191.4 3.7 copy.181
  195.4 1.0 copy.184
  196.4 1.0 copy.185
  197.4 1.5 broadcast_in_dim.107
  198.9 2.3 broadcast_in_dim.118
  201.1 3.5 copy.179
  204.7 1.5 broadcast_in_dim.104
  206.2 2.3 broadcast_in_dim.113
  208.5 3.7 copy.178
  212.2 4.6 %multiply_reduce_fusion = f32[2048]{0:T(1024)S(1)} fusion(f32[1,384,2048]{1,2,0:T(8,128)} %copy.181, f32[1,384,2048]{1,2,0:T(8,128)} %copy.179, f32[1,384,2048]{1,2,0:T(8,128)} %copy.178, pred[384]{0:T(512)(128)(4,1)S(1)} %broadcast_bitcast_fusion.1, pred[384]{0:T(512)(128)(4,1)S(1)} %broadcast_bitcast_fusion.2, bf16[1,384,2048]{1,2,0:T(8,128)(2,1)S(1)} %copy-done.1), kind=kLoop, calls=%fused_computation.8 | loop fusion | flops 5502976 | bytes 11019008 | tf_op jit(solution)/shard_map/reduce_sum | solution.py:134
  216.9 88.1 %psum.7 = f32[2,128]{1,0:T(2,128)S(1)} all-reduce(f32[2,128]{1,0:T(2,128)S(1)} %pad_maximum_fusion.16), channel_id=1, replica_groups=mesh['song'=4,'seq'=64] {'song','seq'}, use_global_device_ids=true, to_apply=%region_14.15 | all-reduce | flops 256 | bytes 2048 | tf_op jit(solution)/shard_map/psum | solution.py:172
  305.5 90.2 %all-reduce.3.cloned.1.call-done = f32[2,64,12288]{2,0,1:T(2,128)} async-done(((f32[2,64,12288]{2,0,1:T(2,128)}), f32[2,64,12288]{2,0,1:T(2,128)}) %all-reduce.3.cloned.1.call-update) | async-done | bytes 6291472
  396.2 2.3 fusion.38
  398.8 1.7 fusion.28
  400.5 0.7 convert_element_type.177
  401.2 0.6 fusion.25
  (95 shorter events, 6.3 us)
Async XLA Ops:
  7.2 85.4 %all-gather.2.cloned.1.call-start = ((), (), s32[]{:S(2)}) async-start(), calls=%async_computation | async-start | bytes 3194880 | tf_op jit(solution)/shard_map/all_gather | solution.py:89
  9.6 386.1 %all-reduce.3.cloned.1.call-start = ((), (), s32[]{:S(2)}) async-start(), calls=%async_computation.1 | async-start | bytes 12582912
  10.9 9.0 %copy-start.19 = (s32[1,1,2]{2,1,0:T(1,128)S(1)}, s32[1,1,2]{2,1,0:T(1,128)}, u32[]{:S(2)}) copy-start(s32[1,1,2]{2,1,0:T(1,128)} %param.34) | copy-start | bytes 28
  11.0 12.2 %copy-start.12 = (bf16[1,128,2048]{2,1,0:T(8,128)(2,1)S(1)}, bf16[1,128,2048]{2,1,0:T(8,128)(2,1)}, u32[]{:S(2)}) copy-start(bf16[1,128,2048]{2,1,0:T(8,128)(2,1)} %param.33) | copy-start | bytes 1572868
  14.6 11.6 %collective-permute-start.1 = (bf16[2,128,2048]{1,2,0:T(8,128)(2,1)S(1)}, bf16[2,128,2048]{1,2,0:T(8,128)(2,1)}, u32[]{:S(2)}, u32[]{:S(2)}) collective-permute-start(bf16[2,128,2048]{1,2,0:T(8,128)(2,1)S(1)} %pad_maximum_fusion.9), channel_id=1, source_target_pairs={{1,0},{2,1},{3,2},{4,3},{5,4},{6,5},{7,6},{8,7},{9,8},{10,9},{11,1... | collective-permute-start | bytes 3145736 | tf_op jit(solution)/shard_map/ppermute | solution.py:20
  15.9 10.3 %collective-permute-start = (bf16[2,128,2048]{1,2,0:T(8,128)(2,1)S(1)}, bf16[2,128,2048]{1,2,0:T(8,128)(2,1)}, u32[]{:S(2)}, u32[]{:S(2)}) collective-permute-start(bf16[2,128,2048]{1,2,0:T(8,128)(2,1)S(1)} %pad_maximum_fusion.9), channel_id=1, source_target_pairs={{0,1},{1,2},{2,3},{3,4},{4,5},{5,6},{6,7},{7,8},{8,9},{9,10},{10,1... | collective-permute-start | bytes 3145736 | tf_op jit(solution)/shard_map/ppermute | solution.py:17
  26.0 106.0 %copy-start.2 = (f32[1,128,2048]{1,2,0:T(8,128)}, f32[1,128,2048]{1,2,0:T(8,128)S(1)}, u32[]{:S(2)}) copy-start(f32[1,128,2048]{1,2,0:T(8,128)S(1)} %copy.163) | copy-start | bytes 3145732
  109.1 2.5 copy-start
  111.2 7.3 %copy-start.18 = (f32[128]{0:T(128)S(1)}, f32[128]{0:T(128)}, u32[]{:S(2)}) copy-start(f32[128]{0:T(128)} %param.32) | copy-start | bytes 1540
  120.9 1.8 copy-start.9
  121.0 1.8 copy-start.20
  121.1 3.2 copy-start.15
  121.1 3.2 copy-start.16
  122.7 1.6 copy-start.14
  124.3 3.1 copy-start.11
  132.1 3.3 copy-start.7
  136.1 7.2 %copy-start.21 = (u32[256]{0:T(256)S(1)}, u32[256]{0:T(256)}, u32[]{:S(2)}) copy-start(u32[256]{0:T(256)} %constant.174) | copy-start | bytes 3076
  136.3 12.3 %slice-start = ((s8[5242880]{0:T(1024)(128)(4,1)}), s8[1048576]{0:T(1024)(128)(4,1)S(1)}, s32[]{:S(2)}) async-start(s8[5242880]{0:T(1024)(128)(4,1)} %bitcast.106), calls=%async_computation.2 | async-start | bytes 2097152
  138.0 7.3 %collective-permute-start.3 = (bf16[2,128,2048]{1,2,0:T(8,128)(2,1)}, bf16[2,128,2048]{1,2,0:T(8,128)(2,1)}, u32[]{:S(2)}, u32[]{:S(2)}) collective-permute-start(bf16[2,128,2048]{1,2,0:T(8,128)(2,1)} %get-tuple-element.176), channel_id=1, source_target_pairs={{1,0},{2,1},{3,2},{4,3},{5,4},{6,5},{7,6},{8,7},{9,8},{10,9},{11,1... | collective-permute-start | bytes 3145736 | tf_op jit(solution)/shard_map/ppermute | solution.py:20
  139.3 6.0 %collective-permute-start.2 = (bf16[2,128,2048]{1,2,0:T(8,128)(2,1)}, bf16[2,128,2048]{1,2,0:T(8,128)(2,1)}, u32[]{:S(2)}, u32[]{:S(2)}) collective-permute-start(bf16[2,128,2048]{1,2,0:T(8,128)(2,1)} %get-tuple-element.175), channel_id=1, source_target_pairs={{0,1},{1,2},{2,3},{3,4},{4,5},{5,6},{6,7},{7,8},{8,9},{9,10},{10,1... | collective-permute-start | bytes 3145736 | tf_op jit(solution)/shard_map/ppermute | solution.py:17
  145.3 3.3 slice-start.1
  145.3 3.7 copy-start.4
  181.5 0.8 copy-start.17
  181.5 1.1 copy-start.13
  181.5 2.1 copy-start.3
  181.5 2.1 copy-start.10
  191.3 3.7 copy-start.5
  191.3 3.7 copy-start.6
  195.0 1.4 copy-start.8
  208.5 3.7 copy-start.1
Sparse Core Ops, SparseCore 0:
  11.3 81.1 all-gather.1
  181.6 213.9 all-reduce.2
where the time goes:
time: 410 us; the launch traced here: 409 us
  waiting for transfers between devices  152 us (37%)
  local copies, waits for them, and re-layouts  91.8 us (22%)
  blocking collectives  88.1 us (21%)
  other arithmetic  32.9 us (8%)
  between operations  17.9 us (4%)
  matrix products  15.8 us (4%)
  starting transfers between devices  10.7 us (3%)
    unnamed x3, waiting for transfers between devices  90.2 us
    psum x1, blocking collectives, body(): lax.psum(jnp.stack([query_gain_vector, key_gain_vector + lyric_gain_vecto...  88.1 us
    all_gather x1, waiting for transfers between devices, body(): lyric_all = lax.all_gather(lyric_pair, 'seq', axis=1, tiled=True)  61.3 us
    unnamed x59, local copies, waits for them, and re-layouts  19.6 us
    broadcast_in_dim x8, local copies, waits for them, and re-layouts, body(): jnp.where(pick[s], lyric_gk[s][None], 0.0)  15 us
    slice x1, local copies, waits for them, and re-layouts, body(): lyric_raw_all = lyric_all[0]  9.57 us
  transfers between devices with their start and end apart: 6, of which 2 were waited for; matrix products, arithmetic and copies ran while one was open for 12% of the time, Pallas kernels for 0%

commit v1 on v0

--- a/solution.py
+++ b/solution.py
@@ -1,3 +1,4 @@
+import functools
 import jax
 import jax.numpy as jnp
 from jax import lax
@@ -7,6 +8,16 @@
 WIN = 1
 TILES = 2
 NORM_EPS = 1e-06
+
+
+def obtain_heads_on_mesh(x_local, along_dim):
+    return jnp.concatenate(
+        lax.all_to_all(jnp.stack(lax.psum(1, "seq") * [x_local], axis=0), "seq", 0, 0),
+        axis=along_dim,
+    )
+
+
+_open_forms = functools.partial(obtain_heads_on_mesh, along_dim=1)
 
 
 def extended_2(block, sides, width):
@@ -86,7 +97,7 @@
     lyric_total = lyric_local * seq_count
     lyric_blocks = lyric_total // BLK
     lyric_pair = jnp.stack([lyric_keys[0], lyric_values[0]])
-    lyric_all = lax.all_gather(lyric_pair, "seq", axis=1, tiled=True)
+    lyric_all = _open_forms(lyric_pair)
     lyric_raw_all = lyric_all[0]
     lyric_val_all = lyric_all[1].reshape(lyric_total, head_count, head_size)
     query_raw = queries[0]

time: 410 us -> 423 us (1.032)
  local copies, waits for them, and re-layouts: 91.8 us -> 58.1 us
  other arithmetic: 32.9 us -> 50.1 us
  blocking collectives: 88.1 us -> 103 us
  starting transfers between devices: 10.7 us -> 23 us
    all_gather x1 -> x0, waiting for transfers between devices: 61.3 us -> none  [body(): lyric_all = lax.all_gather(lyric_pair, 'seq', axis=1, tiled=True)]
    all_to_all x0 -> x1, waiting for transfers between devices: none -> 54.8 us  [obtain_heads_on_mesh(): lax.all_to_all(jnp.stack(lax.psum(1, 'seq') * [x_local], axis=0), 'seq',...]
    slice x2 -> x0, local copies, waits for them, and re-layouts: 16.5 us -> none  [the longest x1 9.57 us: body(): lyric_raw_all = lyric_all[0]]
    psum x1, blocking collectives: 88.1 us -> 103 us  [body(): lax.psum(jnp.stack([query_gain_vector, key_gain_vector + lyric_gain_vecto...]
    all_to_all x0 -> x1, starting transfers between devices: none -> 12.3 us  [obtain_heads_on_mesh(): lax.all_to_all(jnp.stack(lax.psum(1, 'seq') * [x_local], axis=0), 'seq',...]
    unnamed x59 -> x50, local copies, waits for them, and re-layouts: 19.6 us -> 9.28 us
    unnamed x3 -> x2, waiting for transfers between devices: 90.2 us -> 97.8 us
    another operation x1, other arithmetic: 3.29 us -> 10.8 us  [body(): jnp.stack([part_gk, part_gv])]
  transfers between devices with their start and end apart: 6 -> 6, of which waited for: 2 -> 2; matrix products, arithmetic and copies ran while one was open for 12% -> 9% of each run, Pallas kernels for 0% -> 0%
where the time goes in v1:
time: 423 us; the launch traced here: 422 us
  waiting for transfers between devices  153 us (36%)
  blocking collectives  103 us (24%)
  local copies, waits for them, and re-layouts  58.1 us (14%)
  other arithmetic  50.1 us (12%)
  starting transfers between devices  23 us (5%)
  between operations  17.9 us (4%)
  matrix products  17.4 us (4%)
    psum x1, blocking collectives, body(): lax.psum(jnp.stack([query_gain_vector, key_gain_vector + lyric_gain_vecto...  103 us
    unnamed x2, waiting for transfers between devices  97.8 us
    all_to_all x1, waiting for transfers between devices, obtain_heads_on_mesh(): lax.all_to_all(jnp.stack(lax.psum(1, 'seq') * [x_local], axis=0), 'seq',...  54.8 us
    all_to_all x1, starting transfers between devices, obtain_heads_on_mesh(): lax.all_to_all(jnp.stack(lax.psum(1, 'seq') * [x_local], axis=0), 'seq',...  12.3 us
    another operation x1, other arithmetic, body(): jnp.stack([part_gk, part_gv])  10.8 us
    unnamed x50, local copies, waits for them, and re-layouts  9.28 us
  transfers between devices with their start and end apart: 6, of which 2 were waited for; matrix products, arithmetic and copies ran while one was open for 9% of the time, Pallas kernels for 0%

profile of v1, /device:TPU:8, one launch (start us, length us, event | category | flops | bytes accessed | tf_op | source)
XLA Modules:
  0.0 422.2 jit_solution(11906015357980051999)
XLA Ops:
  7.2 0.8 pad_maximum_fusion.15
  8.0 4.7 %stack.17 = bf16[64,2,6,2048]{3,1,2,0:T(2,128)(2,1)} broadcast(bf16[2,6,2048]{2,0,1:T(2,128)(2,1)S(1)} %copy.163), dimensions={1,2,3} | broadcast | bytes 3194880 | tf_op jit(solution)/shard_map/stack | solution.py:15
  12.7 12.3 %all-to-all-start = ((bf16[64,2,6,2048]{3,1,2,0:T(2,128)(2,1)}), bf16[64,2,6,2048]{3,1,2,0:T(2,128)(2,1)}, u32[]{:S(2)}, u32[]{:S(2)}) async-start(bf16[64,2,6,2048]{3,1,2,0:T(2,128)(2,1)} %stack.17), calls=%async_computation | async-start | bytes 6291456 | tf_op jit(solution)/shard_map/all_to_all | solution.py:15
  25.7 1.1 multiply_reduce_fusion.6
  27.3 1.3 collective-permute-start.1
  28.6 4.0 collective-permute-start
  32.6 0.6 fusion.47
  35.8 1.0 copy.172
  37.5 1.2 copy.167
  38.9 1.9 pad_maximum_fusion.1
  40.9 1.5 fusion.44
  42.4 1.6 copy.170
  44.0 54.8 %all-to-all-done = bf16[64,2,6,2048]{3,1,2,0:T(2,128)(2,1)} async-done(((bf16[64,2,6,2048]{3,1,2,0:T(2,128)(2,1)}), bf16[64,2,6,2048]{3,1,2,0:T(2,128)(2,1)}, u32[]{:S(2)}, u32[]{:S(2)}) %all-to-all-start) | async-done | bytes 3145760 | tf_op jit(solution)/shard_map/all_to_all | solution.py:15
  98.8 3.5 copy.203
  102.3 3.7 slice_convert_fusion
  106.3 3.4 reshape.558
  109.7 0.9 multiply_reduce_fusion.1
  110.7 2.7 fusion.4
  113.3 3.5 reshape_squeeze.19
  116.9 2.4 constant_dynamic-slice_fusion.1
  119.2 1.0 constant_dynamic-slice_fusion.3
  120.2 1.5 copy.193
  122.2 3.1 fusion.2
  125.4 3.1 fusion.49
  128.5 2.4 multiply_reduce_fusion.4
  130.9 2.1 fusion
  133.1 3.3 fusion.48
  137.3 1.7 fusion.13
  139.0 1.3 collective-permute-start.3
  140.3 4.0 collective-permute-start.2
  144.3 1.3 iota_compare_fusion
  146.1 0.6 dynamic-slice.20
  146.7 3.2 maximum_convert_fusion
  149.9 3.6 fusion.42
  153.5 0.5 copy.178
  154.0 2.1 copy.177
  156.2 4.5 %fusion.43 = (f32[128,16,128]{0,2,1:T(8,128)}, f32[128,16,128]{0,2,1:T(8,128)}, bf16[128,16,128]{0,2,1:T(8,128)(2,1)}) fusion(f32[640,16,128]{0,2,1:T(8,128)} %get-tuple-element.195, f32[128,16,128]{0,2,1:T(8,128)} %bitcast.109, f32[128,16,128]{0,2,1:T(8,128)} %bitcast.108), kind=kLoop, calls=%fused_computation.109 | loop fusion | flops 786432 | bytes 7864320 | tf_op jit(solution)/shard_map/slice | solution.py:141
  160.7 2.6 copy.180
  163.3 2.6 copy.179
  165.9 3.9 select_add_fusion.1
  169.8 10.8 %pad_maximum_fusion = f32[2,64,12288]{2,0,1:T(2,128)} fusion(f32[1,64,12288]{2,0,1:T(1,128)} %bitcast.101, f32[1,64,12288]{2,0,1:T(1,128)S(1)} %bitcast.100), kind=kLoop, calls=%fused_computation | loop fusion | flops 1572864 | bytes 12582912 | tf_op jit(solution)/shard_map/stack | solution.py:146
  180.8 0.9 copy-done.13
  181.6 1.0 copy.182
  182.6 3.2 fusion.18
  185.9 0.6 fusion.20
  186.5 1.0 copy.183
  187.5 0.9 mul.399
  188.4 2.2 mul.400
  190.6 1.9 subtract_convert_fusion
  192.5 1.0 copy.184
  193.5 1.0 copy.185
  194.5 1.5 broadcast_in_dim.107
  196.0 2.2 broadcast_in_dim.118
  198.2 1.5 broadcast_in_dim.104
  199.7 2.2 broadcast_in_dim.113
  201.9 5.9 %multiply_reduce_fusion = f32[2048]{0:T(1024)S(1)} fusion(f32[1,64,6,2048]{3,2,1,0:T(8,128)} %mul.400, f32[1,64,6,2048]{3,2,1,0:T(8,128)} %broadcast_in_dim.118, f32[1,64,6,2048]{3,2,1,0:T(8,128)} %broadcast_in_dim.113, pred[64,6]{1,0:T(8,128)(4,1)S(1)} %broadcast_in_dim.116, pred[64,6]{1,0:T(8,128)(4,1)S(1)} %broadcast_in_dim.111, ...), kind=kLoop, calls=%fused_computation.8 | loop fusion | flops 5502976 | bytes 11019008 | tf_op jit(solution)/shard_map/reduce_sum | solution.py:145
  207.8 103.1 %psum.7 = f32[2,128]{1,0:T(2,128)S(1)} all-reduce(f32[2,128]{1,0:T(2,128)S(1)} %pad_maximum_fusion.16), channel_id=1, replica_groups=mesh['song'=4,'seq'=64] {'song','seq'}, use_global_device_ids=true, to_apply=%region_14.15 | all-reduce | flops 256 | bytes 2048 | tf_op jit(solution)/shard_map/psum | solution.py:183
  310.9 0.5 slice_bitcast_fusion
  311.4 97.8 %all-reduce.3.cloned.1.call-done = f32[2,64,12288]{2,0,1:T(2,128)} async-done(((f32[2,64,12288]{2,0,1:T(2,128)}), f32[2,64,12288]{2,0,1:T(2,128)}) %all-reduce.3.cloned.1.call-update) | async-done | bytes 6291472
  409.2 0.5 broadcast.400
  409.7 2.3 fusion.40
  412.4 1.7 fusion.30
  414.1 0.7 convert_element_type.177
  414.7 0.6 fusion.27
  (84 shorter events, 3.9 us)
Async XLA Ops:
  12.7 12.4 %copy-start.10 = (bf16[1,128,2048]{2,1,0:T(8,128)(2,1)S(1)}, bf16[1,128,2048]{2,1,0:T(8,128)(2,1)}, u32[]{:S(2)}) copy-start(bf16[1,128,2048]{2,1,0:T(8,128)(2,1)} %param.28) | copy-start | bytes 1572868
  12.7 12.6 %copy-start.11 = (bf16[1,128,2048]{2,1,0:T(8,128)(2,1)S(1)}, bf16[1,128,2048]{2,1,0:T(8,128)(2,1)}, u32[]{:S(2)}) copy-start(bf16[1,128,2048]{2,1,0:T(8,128)(2,1)} %param.27) | copy-start | bytes 1572868
  12.7 12.9 %copy-start.16 = (f32[128]{0:T(128)S(1)}, f32[128]{0:T(128)}, u32[]{:S(2)}) copy-start(f32[128]{0:T(128)} %param.32) | copy-start | bytes 1540
  12.7 86.0 %all-to-all-start = ((bf16[64,2,6,2048]{3,1,2,0:T(2,128)(2,1)}), bf16[64,2,6,2048]{3,1,2,0:T(2,128)(2,1)}, u32[]{:S(2)}, u32[]{:S(2)}) async-start(bf16[64,2,6,2048]{3,1,2,0:T(2,128)(2,1)} %stack.17), calls=%async_computation | async-start | bytes 6291456 | tf_op jit(solution)/shard_map/all_to_all | solution.py:15
  25.1 384.2 %all-reduce.3.cloned.1.call-start = ((), (), s32[]{:S(2)}) async-start(), calls=%async_computation.1 | async-start | bytes 12582912
  25.4 7.2 %copy-start.17 = (s32[1,1,2]{2,1,0:T(1,128)S(1)}, s32[1,1,2]{2,1,0:T(1,128)}, u32[]{:S(2)}) copy-start(s32[1,1,2]{2,1,0:T(1,128)} %param.34) | copy-start | bytes 28
  25.7 10.1 %copy-start.12 = (bf16[1,128,2048]{2,1,0:T(8,128)(2,1)S(1)}, bf16[1,128,2048]{2,1,0:T(8,128)(2,1)}, u32[]{:S(2)}) copy-start(bf16[1,128,2048]{2,1,0:T(8,128)(2,1)} %param.33) | copy-start | bytes 1572868
  27.3 11.6 %collective-permute-start.1 = (bf16[2,128,2048]{1,2,0:T(8,128)(2,1)S(1)}, bf16[2,128,2048]{1,2,0:T(8,128)(2,1)}, u32[]{:S(2)}, u32[]{:S(2)}) collective-permute-start(bf16[2,128,2048]{1,2,0:T(8,128)(2,1)S(1)} %pad_maximum_fusion.9), channel_id=1, source_target_pairs={{1,0},{2,1},{3,2},{4,3},{5,4},{6,5},{7,6},{8,7},{9,8},{10,9},{11,1... | collective-permute-start | bytes 3145736 | tf_op jit(solution)/shard_map/ppermute | solution.py:31
  28.6 10.3 %collective-permute-start = (bf16[2,128,2048]{1,2,0:T(8,128)(2,1)S(1)}, bf16[2,128,2048]{1,2,0:T(8,128)(2,1)}, u32[]{:S(2)}, u32[]{:S(2)}) collective-permute-start(bf16[2,128,2048]{1,2,0:T(8,128)(2,1)S(1)} %pad_maximum_fusion.9), channel_id=1, source_target_pairs={{0,1},{1,2},{2,3},{3,4},{4,5},{5,6},{6,7},{7,8},{8,9},{9,10},{10,1... | collective-permute-start | bytes 3145736 | tf_op jit(solution)/shard_map/ppermute | solution.py:28
  38.7 2.1 copy-start.1
  102.3 4.0 copy-start
  116.8 5.3 %copy-start.2 = (f32[1,128,2048]{1,2,0:T(8,128)S(1)}, f32[1,128,2048]{1,2,0:T(8,128)}, u32[]{:S(2)}) copy-start(f32[1,128,2048]{1,2,0:T(8,128)} %copy-done.1) | copy-start | bytes 3145732
  116.9 5.3 %copy-start.18 = (f32[128]{0:T(128)S(1)}, f32[128]{0:T(128)}, u32[]{:S(2)}) copy-start(f32[128]{0:T(128)} %param.31) | copy-start | bytes 1540
  122.2 3.2 copy-start.14
  125.3 3.1 copy-start.9
  133.1 3.3 copy-start.6
  137.1 9.0 %copy-start.19 = (u32[256]{0:T(256)S(1)}, u32[256]{0:T(256)}, u32[]{:S(2)}) copy-start(u32[256]{0:T(256)} %constant.174) | copy-start | bytes 3076
  137.1 9.6 %copy-start.15 = (bf16[1,6,2048]{2,1,0:T(8,128)(2,1)S(1)}, bf16[1,6,2048]{2,1,0:T(8,128)(2,1)}, u32[]{:S(2)}) copy-start(bf16[1,6,2048]{2,1,0:T(8,128)(2,1)} %param.29) | copy-start | bytes 73732
  139.0 7.7 %collective-permute-start.3 = (bf16[2,128,2048]{1,2,0:T(8,128)(2,1)}, bf16[2,128,2048]{1,2,0:T(8,128)(2,1)}, u32[]{:S(2)}, u32[]{:S(2)}) collective-permute-start(bf16[2,128,2048]{1,2,0:T(8,128)(2,1)} %get-tuple-element.176), channel_id=1, source_target_pairs={{1,0},{2,1},{3,2},{4,3},{5,4},{6,5},{7,6},{8,7},{9,8},{10,9},{11,1... | collective-permute-start | bytes 3145736 | tf_op jit(solution)/shard_map/ppermute | solution.py:31
  140.3 6.4 %collective-permute-start.2 = (bf16[2,128,2048]{1,2,0:T(8,128)(2,1)}, bf16[2,128,2048]{1,2,0:T(8,128)(2,1)}, u32[]{:S(2)}, u32[]{:S(2)}) collective-permute-start(bf16[2,128,2048]{1,2,0:T(8,128)(2,1)} %get-tuple-element.175), channel_id=1, source_target_pairs={{0,1},{1,2},{2,3},{3,4},{4,5},{5,6},{6,7},{7,8},{8,9},{9,10},{10,1... | collective-permute-start | bytes 3145736 | tf_op jit(solution)/shard_map/ppermute | solution.py:28
  146.7 3.2 copy-start.3
  154.0 11.8 %copy-start.5 = (f32[128,16,128]{2,1,0:T(8,128)}, f32[128,16,128]{2,1,0:T(8,128)S(1)}, u32[]{:S(2)}) copy-start(f32[128,16,128]{2,1,0:T(8,128)S(1)} %copy.178) | copy-start | bytes 3145732
  156.1 9.7 %copy-start.4 = (f32[128,16,128]{2,1,0:T(8,128)}, f32[128,16,128]{2,1,0:T(8,128)S(1)}, u32[]{:S(2)}) copy-start(f32[128,16,128]{2,1,0:T(8,128)S(1)} %copy.177) | copy-start | bytes 3145732
  180.6 1.0 copy-start.13
  180.6 2.0 copy-start.8
  190.6 2.9 copy-start.7
Sparse Core Ops, SparseCore 0:
  180.7 228.4 all-reduce.2
